TPU v7x, 256 devices: a whole 4x4x8 slice. The times are simulated.
256 devices in a mesh: px: 4 (over z_lo), py: 8 (over y, core), ch: 8 (over z_hi, x).
Axes of the slice: x: 4, y: 4, z: 8 (z_hi: 2, z_lo: 4; z = z_hi * 4 + z_lo), core: 2. Of those that a mesh axis runs over, the one named last changes fastest.
Arguments:
- features: bfloat16 [128, 12, 8, 4, 512], P('ch', None, 'py', 'px'), may hold values from -6 to 6
- cotangent: bfloat16 [128, 12, 8, 4, 512], P('ch', None, 'py', 'px'), may hold values from -6 to 6
- weight: bfloat16 [3, 3, 128, 128], replicated, may hold values from -0.1875 to 0.1875
- edge_table: int32 [12, 4, 3], replicated, may hold values from 0 to 11, as said below
- corner_table: int32 [12, 4, 2], replicated, may hold values from 0 to 11, as said below
Outputs:
- activation: bfloat16 [128, 12, 8, 4, 512], P('ch', None, 'py', 'px')
- input_grad: bfloat16 [128, 12, 8, 4, 512], P('ch', None, 'py', 'px')
Inputs may be any that keep to these rules, and one draw needn't show every extreme that they name: edge_table[f, e] = (g, s, r): beyond edge e of face f lie the pixels of side s of face g, in reverse order if r = 1; every side of every face is named exactly once, and if (f, e) names (g, s) then (g, s) names (f, e) with the same r. corner_table[f, c] = (h, q): corner c of face f takes corner pixel q of face h; in each corner column every face appears once, and each q appears 12 times.
All inputs are finite; a program needn't handle non-finite values.
Results may differ from a plain program's by a relative error of at most 0.0049.
Values may be sent and summed in bfloat16 or wider, within the bound.
A program may use at most 192 MiB of HBM per device.

v0:
```python
import jax
import jax.numpy as jnp
from jax import lax
from jax.sharding import PartitionSpec as P

RB = 32


def with_halo(array, sides, width):
    for axis, dim in sides:
        size, length = (lax.axis_size(axis), array.shape[dim])
        up = [(i, (i + 1) % size) for i in range(size - 1)]
        down = [(j, i) for i, j in up]
        last = lax.slice_in_dim(array, length - width, length, axis=dim)
        leading = lax.slice_in_dim(array, 0, width, axis=dim)
        before = lax.ppermute(last, axis, up)
        after = lax.ppermute(leading, axis, down)
        array = jnp.concatenate([before, array, after], axis=dim)
    return array


def edge_strips(lines, edge_table, corner_table):
    chan_count = lines.shape[0]
    face_count = lines.shape[1]
    side_len = lines.shape[3]
    flat_lines = lines.reshape(chan_count, face_count * 4, side_len)
    pixels = jnp.stack(
        [lines[:, :, 0, 0], lines[:, :, 0, -1], lines[:, :, 1, 0], lines[:, :, 1, -1]], axis=2
    ).reshape(chan_count, face_count * 4)
    corner_index = corner_table[:, :, 0] * 4 + corner_table[:, :, 1]
    corner_vals = jnp.take(pixels, corner_index, axis=1)
    strips = []
    for edge_num, start_corner, end_corner in ((0, 0, 1), (1, 2, 3), (2, 0, 2), (3, 1, 3)):
        source_row = edge_table[:, edge_num, 0] * 4 + edge_table[:, edge_num, 1]
        strip_line = jnp.take(flat_lines, source_row, axis=1)
        flipped = (edge_table[:, edge_num, 2] == 1)[None, :, None]
        strip_line = jnp.where(flipped, strip_line[:, :, ::-1], strip_line)
        strips.append(
            jnp.concatenate(
                [
                    corner_vals[:, :, start_corner : start_corner + 1],
                    strip_line,
                    corner_vals[:, :, end_corner : end_corner + 1],
                ],
                axis=2,
            )
        )
    return strips


def face_lines_of(field, row_pos, col_pos, px_count, py_count):
    chan_block = field.shape[0]
    face_count = field.shape[1]
    col_len = field.shape[2]
    row_len = field.shape[3]
    side_len = row_len * px_count
    blank = jnp.zeros((chan_block, face_count, side_len), jnp.float32)

    def placed(values, offset, active):
        return jnp.where(
            active,
            lax.dynamic_update_slice_in_dim(blank, values.astype(jnp.float32), offset, 2),
            0.0,
        )

    contrib = jnp.stack(
        [
            placed(field[:, :, 0, :], row_pos * row_len, col_pos == 0),
            placed(field[:, :, -1, :], row_pos * row_len, col_pos == py_count - 1),
            placed(field[:, :, :, 0], col_pos * col_len, row_pos == 0),
            placed(field[:, :, :, -1], col_pos * col_len, row_pos == px_count - 1),
        ],
        axis=2,
    )
    return lax.psum(contrib.astype(jnp.bfloat16), ("px", "py"))


def pad_field(field, edge_table, corner_table):
    col_len = field.shape[2]
    row_len = field.shape[3]
    row_pos = lax.axis_index("px")
    col_pos = lax.axis_index("py")
    px_count = lax.axis_size("px")
    py_count = lax.axis_size("py")
    padded = with_halo(field, (("px", 3), ("py", 2)), 1)
    lines = face_lines_of(field, row_pos, col_pos, px_count, py_count)
    strips = edge_strips(lines, edge_table, corner_table)
    top_row = lax.dynamic_slice_in_dim(strips[0], row_pos * row_len, row_len + 2, 2)
    bottom_row = lax.dynamic_slice_in_dim(strips[1], row_pos * row_len, row_len + 2, 2)
    left_col = lax.dynamic_slice_in_dim(strips[2], col_pos * col_len, col_len + 2, 2)
    right_col = lax.dynamic_slice_in_dim(strips[3], col_pos * col_len, col_len + 2, 2)
    padded = padded.at[:, :, 0, :].set(jnp.where(col_pos == 0, top_row, padded[:, :, 0, :]))
    padded = padded.at[:, :, -1, :].set(
        jnp.where(col_pos == py_count - 1, bottom_row, padded[:, :, -1, :])
    )
    padded = padded.at[:, :, :, 0].set(jnp.where(row_pos == 0, left_col, padded[:, :, :, 0]))
    padded = padded.at[:, :, :, -1].set(
        jnp.where(row_pos == px_count - 1, right_col, padded[:, :, :, -1])
    )
    return padded


def forward_taps(padded, taps, out_cols, out_rows):
    summed = None
    for tap_row in range(3):
        for tap_col in range(3):
            window = padded[:, :, tap_row : tap_row + out_cols, tap_col : tap_col + out_rows]
            term_val = jnp.einsum(
                "oc,cfab->ofab", taps[tap_row, tap_col], window, preferred_element_type=jnp.float32
            )
            summed = term_val if summed is None else summed + term_val
    return summed


def backward_taps(padded, taps, out_cols, out_rows):
    summed = None
    for tap_row in range(3):
        for tap_col in range(3):
            window = padded[
                :, :, 2 - tap_row : 2 - tap_row + out_cols, 2 - tap_col : 2 - tap_col + out_rows
            ]
            term_val = jnp.einsum(
                "oc,ofab->cfab", taps[tap_row, tap_col], window, preferred_element_type=jnp.float32
            )
            summed = term_val if summed is None else summed + term_val
    return summed


def gate_outputs(preact, cotangent):
    sigmoid_val = jax.nn.sigmoid(preact)
    activation = (preact * sigmoid_val).astype(jnp.bfloat16)
    gated = (
        cotangent.astype(jnp.float32) * sigmoid_val * (1.0 + preact * (1.0 - sigmoid_val))
    ).astype(jnp.bfloat16)
    return (activation, gated)


def local(features, cotangent, weight, edge_table, corner_table):
    chan_block = features.shape[0]
    face_count = features.shape[1]
    tile_len = features.shape[4]
    row_len = RB
    col_len = tile_len // row_len
    features = features.reshape(chan_block, face_count, col_len, row_len)
    cotangent = cotangent.reshape(chan_block, face_count, col_len, row_len)
    ch_pos = lax.axis_index("ch")
    feat_pad = pad_field(features, edge_table, corner_table)
    own_taps = lax.dynamic_slice_in_dim(weight, ch_pos * chan_block, chan_block, 2)
    piece_taps = own_taps
    preact = forward_taps(
        lax.all_gather(feat_pad, "ch", axis=0, tiled=True), piece_taps, col_len, row_len
    )
    activation, gated = gate_outputs(preact, cotangent)
    grad_pad = pad_field(gated, edge_table, corner_table)
    input_taps = lax.dynamic_slice_in_dim(weight, ch_pos * chan_block, chan_block, 3)
    piece_taps = input_taps
    input_grad = backward_taps(
        lax.all_gather(grad_pad, "ch", axis=0, tiled=True), piece_taps, col_len, row_len
    ).astype(jnp.bfloat16)
    out_shape = (chan_block, face_count, 1, 1, tile_len)
    return (activation.reshape(out_shape), input_grad.reshape(out_shape))


def solution(mesh):
    return jax.shard_map(
        local,
        mesh=mesh,
        in_specs=(P("ch", None, "py", "px", None), P("ch", None, "py", "px", None), P(), P(), P()),
        out_specs=(P("ch", None, "py", "px", None), P("ch", None, "py", "px", None)),
        check_vma=False,
    )
```

profile of v0, /device:TPU:8, one launch (start us, length us, event | category | flops | bytes accessed | tf_op | source)
XLA Modules:
  0.0 1055.1 jit_solution(10775510683861696942)
XLA Ops:
  7.2 1.4 reshape.426
  9.9 1.4 convert_select_fusion.2
  11.2 3.0 copy.696
  14.2 1.8 copy.697
  16.1 2.7 select_n.196
  18.7 2.7 select_n.200
  23.1 2.6 copy.698
  27.0 7.1 collective-permute-start
  39.3 1.6 copy.687
  41.3 1.6 copy.689
  43.6 1.9 collective-permute-start.2
  45.5 3.9 collective-permute-start.3
  49.5 1.4 collective-permute-done.3
  51.5 1.6 pad_maximum_fusion
  53.1 254.8 %all-reduce.3.cloned.1.call-done = bf16[16,12,4,128]{1,0,3,2:T(8,128)(2,1)} async-done(((bf16[16,12,4,128]{1,0,3,2:T(8,128)(2,1)}), bf16[16,12,4,128]{1,0,3,2:T(8,128)(2,1)}) %all-reduce.3.cloned.1.call-update) | async-done | bytes 196624 | tf_op jit(solution)/shard_map/psum | solution.py:75
  307.9 3.0 copy.702
  318.9 3.8 scatter.30
  326.8 18.3 %scatter.31 = bf16[16,12,18,34]{3,0,2,1:T(8,128)(2,1)S(1)} dynamic-update-slice(bf16[16,12,18,34]{3,0,2,1:T(8,128)(2,1)S(1)} %scatter.30, bf16[16,12,18,1]{3,0,2,1:T(8,128)(2,1)S(1)} %copy.707, s32[]{:T(128)} %constant.235.clone.1, s32[]{:T(128)} %constant.235.clone.1, s32[]{:T(128)} %constant.235.clone.1, s32[]{:T(128)} %constant.249.clone.1) | dynamic-update-slice | bytes 13828 | tf_op jit(solution)/shard_map/scatter | solution.py:97
  347.9 162.8 %all-gather.3.cloned.1.call-done = bf16[128,12,18,34]{3,0,2,1:T(8,128)(2,1)} async-done(((bf16[16,12,18,34]{3,0,2,1:T(8,128)(2,1)}), bf16[128,12,18,34]{3,0,2,1:T(8,128)(2,1)}) %all-gather.3.cloned.1.call-update) | async-done | bytes 1880080 | tf_op jit(solution)/shard_map/all_gather | solution.py:151
  510.7 4.7 fusion.20
  515.5 1.8 fusion.24
  518.3 1.8 fusion.26
  521.0 1.8 fusion.30
  522.8 1.8 fusion.32
  524.6 2.0 fusion.18
  526.6 2.6 fusion.37
  529.2 1.7 convert_select_fusion.1
  531.6 2.3 copy.725
  536.3 2.2 collective-permute-start.4
  541.1 1.9 select_n.220
  543.0 1.9 select_n.223
  545.7 2.6 copy.727
  551.1 1.9 collective-permute-start.6
  553.0 3.9 collective-permute-start.7
  556.9 1.5 collective-permute-done.7
  559.2 266.2 %all-reduce.5.cloned.1.call-done = bf16[16,12,4,128]{1,0,3,2:T(8,128)(2,1)} async-done(((bf16[16,12,4,128]{1,0,3,2:T(8,128)(2,1)}), bf16[16,12,4,128]{1,0,3,2:T(8,128)(2,1)}) %all-reduce.5.cloned.1.call-update) | async-done | bytes 196624 | tf_op jit(solution)/shard_map/psum | solution.py:75
  825.4 3.0 copy.731
  837.1 3.8 scatter.36
  844.2 18.6 %scatter.39 = bf16[16,12,18,34]{3,0,2,1:T(8,128)(2,1)S(1)} dynamic-update-slice(bf16[16,12,18,34]{3,0,2,1:T(8,128)(2,1)S(1)} %scatter.36, bf16[16,12,18,1]{3,0,2,1:T(8,128)(2,1)S(1)} %copy.735, s32[]{:T(128)} %constant.235.clone.1, s32[]{:T(128)} %constant.235.clone.1, s32[]{:T(128)} %constant.235.clone.1, s32[]{:T(128)} %constant.249.clone.1) | dynamic-update-slice | bytes 13828 | tf_op jit(solution)/shard_map/scatter | solution.py:97
  864.1 1.4 reshape.433
  865.5 162.9 %all-gather.5.cloned.1.call-done = bf16[128,12,18,34]{3,0,2,1:T(8,128)(2,1)} async-done(((bf16[16,12,18,34]{3,0,2,1:T(8,128)(2,1)}), bf16[128,12,18,34]{3,0,2,1:T(8,128)(2,1)}) %all-gather.5.cloned.1.call-update) | async-done | bytes 1880080 | tf_op jit(solution)/shard_map/all_gather | solution.py:158
  1028.4 4.8 fusion.2
  1034.3 1.9 fusion.10
  1037.2 1.9 fusion.14
  1039.1 1.9 fusion.4
  1040.9 1.9 fusion.8
  1044.1 2.3 add_convert_fusion
  1046.6 1.4 reshape.440
  (185 shorter events, 54.1 us)
Async XLA Ops:
  7.2 503.6 %copy-start = (bf16[3,3,128,128]{3,2,1,0:T(8,128)(2,1)S(1)}, bf16[3,3,128,128]{3,2,1,0:T(8,128)(2,1)}, u32[]{:S(2)}) copy-start(bf16[3,3,128,128]{3,2,1,0:T(8,128)(2,1)} %param.27) | copy-start | bytes 884740
  7.2 300.8 %all-reduce.3.cloned.1.call-start = ((), (), s32[]{:S(2)}) async-start(), calls=%async_computation | async-start | bytes 4194304 | tf_op jit(solution)/shard_map/psum | solution.py:75
  25.7 10.9 %copy-start.17 = (s32[12,4,3]{0,1,2:T(4,128)S(1)}, s32[12,4,3]{0,1,2:T(4,128)}, u32[]{:S(2)}) copy-start(s32[12,4,3]{0,1,2:T(4,128)} %param.28) | copy-start | bytes 1732
  25.7 12.0 %copy-start.26 = (s32[12,4,2]{0,2,1:T(2,128)S(1)}, s32[12,4,2]{0,2,1:T(2,128)}, u32[]{:S(2)}) copy-start(s32[12,4,2]{0,2,1:T(2,128)} %param.29) | copy-start | bytes 1156
  25.7 485.0 %all-gather.3.cloned.1.call-start = ((), (), s32[]{:S(2)}) async-start(), calls=%async_computation.1 | async-start | bytes 7962624 | tf_op jit(solution)/shard_map/all_gather | solution.py:151
  27.0 12.3 %collective-permute-start = (bf16[16,12,16,1]{2,0,3,1:T(8,128)(2,1)S(1)}, bf16[16,12,16,1]{2,0,3,1:T(8,128)(2,1)S(1)}, u32[]{:S(2)}, u32[]{:S(2)}) collective-permute-start(bf16[16,12,16,1]{2,0,3,1:T(8,128)(2,1)S(1)} %copy.684), channel_id=1, source_target_pairs={{0,64},{64,128},{128,192},{1,65},{65,129},{129,193},{2,66},{66,130... | collective-permute-start | bytes 18440 | tf_op jit(solution)/shard_map/ppermute | solution.py:16
  35.3 6.0 collective-permute-start.1
  43.6 5.9 collective-permute-start.2
  45.5 5.4 collective-permute-start.3
  49.5 1.4 copy-start.10
  50.9 0.6 copy-start.12
  53.1 258.7 %copy-start.15 = (pred[12]{0:T(512)(128)(4,1)S(1)}, pred[12]{0:T(512)(128)(4,1)}, u32[]{:S(2)}) copy-start(pred[12]{0:T(512)(128)(4,1)} %get-tuple-element.166) | copy-start | bytes 40
  53.1 259.6 %copy-start.13 = (pred[12]{0:T(512)(128)(4,1)S(1)}, pred[12]{0:T(512)(128)(4,1)}, u32[]{:S(2)}) copy-start(pred[12]{0:T(512)(128)(4,1)} %get-tuple-element.164) | copy-start | bytes 40
  311.0 4.6 copy-start.20
  311.0 4.7 copy-start.11
  311.0 4.9 copy-start.22
  313.8 3.6 copy-start.24
  322.7 2.5 copy-start.18
  345.1 1.0 copy-start.4
  346.1 479.3 %all-reduce.5.cloned.1.call-start = ((), (), s32[]{:S(2)}) async-start(), calls=%async_computation.2 | async-start | bytes 4194304 | tf_op jit(solution)/shard_map/psum | solution.py:75
  510.7 4.8 copy-start.2
  535.1 9.9 copy-start.7
  535.1 10.2 copy-start.6
  536.3 12.1 %collective-permute-start.4 = (bf16[16,12,16,1]{2,0,3,1:T(8,128)(2,1)S(1)}, bf16[16,12,16,1]{2,0,3,1:T(8,128)(2,1)S(1)}, u32[]{:S(2)}, u32[]{:S(2)}) collective-permute-start(bf16[16,12,16,1]{2,0,3,1:T(8,128)(2,1)S(1)} %copy.720), channel_id=1, source_target_pairs={{0,64},{64,128},{128,192},{1,65},{65,129},{129,193},{2,66},{66,130... | collective-permute-start | bytes 18440 | tf_op jit(solution)/shard_map/ppermute | solution.py:16
  539.8 9.9 collective-permute-start.5
  548.4 480.1 %all-gather.5.cloned.1.call-start = ((), (), s32[]{:S(2)}) async-start(), calls=%async_computation.3 | async-start | bytes 7962624 | tf_op jit(solution)/shard_map/all_gather | solution.py:158
  551.1 5.8 collective-permute-start.6
  553.0 5.4 collective-permute-start.7
  556.9 1.5 copy-start.8
  559.1 272.2 %copy-start.16 = (pred[12]{0:T(512)(128)(4,1)S(1)}, pred[12]{0:T(512)(128)(4,1)}, u32[]{:S(2)}) copy-start(pred[12]{0:T(512)(128)(4,1)} %get-tuple-element.166) | copy-start | bytes 40
  559.2 272.4 %copy-start.25 = (pred[12]{0:T(512)(128)(4,1)S(1)}, pred[12]{0:T(512)(128)(4,1)}, u32[]{:S(2)}) copy-start(pred[12]{0:T(512)(128)(4,1)} %get-tuple-element.162) | copy-start | bytes 40
  559.2 272.5 %copy-start.14 = (pred[12]{0:T(512)(128)(4,1)S(1)}, pred[12]{0:T(512)(128)(4,1)}, u32[]{:S(2)}) copy-start(pred[12]{0:T(512)(128)(4,1)} %get-tuple-element.164) | copy-start | bytes 40
  559.2 272.7 %copy-start.23 = (pred[12]{0:T(512)(128)(4,1)S(1)}, pred[12]{0:T(512)(128)(4,1)}, u32[]{:S(2)}) copy-start(pred[12]{0:T(512)(128)(4,1)} %get-tuple-element.161) | copy-start | bytes 40
  828.4 5.5 copy-start.21
  828.5 5.6 copy-start.9
  840.9 1.8 copy-start.19
  842.9 20.9 %copy-start.5 = (bf16[16,12,16,32]{3,0,2,1:T(8,128)(2,1)S(1)}, bf16[16,12,16,32]{3,0,2,1:T(8,128)(2,1)}, u32[]{:S(2)}) copy-start(bf16[16,12,16,32]{3,0,2,1:T(8,128)(2,1)} %get-tuple-element.139) | copy-start | bytes 589828
  862.8 1.0 copy-start.3
  1028.4 4.8 copy-start.1
Sparse Core Ops, SparseCore 0:
  25.8 282.0 all-reduce.2
  346.2 164.4 all-gather.2
  548.5 276.8 all-reduce.4
  863.9 164.4 all-gather.4
where the time goes:
time: 1060 us
  waiting for transfers between devices  850 us (80%)
  local copies, waits for them, and re-layouts  117 us (11%)
  matrix products  36.3 us (3%)
  starting transfers between devices  24 us (2%)
  between operations  15.2 us (1%)
  other arithmetic  12.9 us (1%)
    psum x2, waiting for transfers between devices, face_lines_of(): return lax.psum(contrib.astype(jnp.bfloat16), ('px', 'py'))  521 us
    all_gather x1, waiting for transfers between devices, local(): lax.all_gather(grad_pad, 'ch', axis=0, tiled=True)  163 us
    all_gather x1, waiting for transfers between devices, local(): lax.all_gather(feat_pad, 'ch', axis=0, tiled=True)  163 us
    scatter x2, local copies, waits for them, and re-layouts, pad_field(): padded.at[:, :, :, -1]  36.9 us
  transfers between devices with their start and end apart: 12, of which 7 were waited for; matrix products, arithmetic and copies ran while one was open for 2% of the time, Pallas kernels for 0%

commit v1 on v0

--- a/solution.py
+++ b/solution.py
@@ -2,6 +2,7 @@
 import jax.numpy as jnp
 from jax import lax
 from jax.sharding import PartitionSpec as P
+from jax.lax import all_gather
 
 RB = 32
 
@@ -72,7 +73,10 @@
         ],
         axis=2,
     )
-    return lax.psum(contrib.astype(jnp.bfloat16), ("px", "py"))
+    cover_floor = lambda own_rows, chip_axis: jnp.sum(
+        all_gather(own_rows, axis_name=chip_axis), axis=0
+    )
+    return cover_floor(contrib.astype(jnp.bfloat16), ("px", "py"))
 
 
 def pad_field(field, edge_table, corner_table):

time: 1060 us -> 626 us (0.59)
  waiting for transfers between devices: 850 us -> 410 us
    psum x2 -> x0, waiting for transfers between devices: 521 us -> none  [face_lines_of(): return lax.psum(contrib.astype(jnp.bfloat16), ('px', 'py'))]
    all_gather x0 -> x2, waiting for transfers between devices: none -> 86.3 us  [face_lines_of(): all_gather(own_rows, axis_name=chip_axis)]
  transfers between devices with their start and end apart: 12 -> 12, of which waited for: 7 -> 10; matrix products, arithmetic and copies ran while one was open for 2% -> 3% of each run, Pallas kernels for 0% -> 0%
where the time goes in v1:
time: 626 us; the launch traced here: 618 us
  waiting for transfers between devices  410 us (65%)
  local copies, waits for them, and re-layouts  107 us (17%)
  matrix products  36.3 us (6%)
  starting transfers between devices  27.2 us (4%)
  other arithmetic  22.8 us (4%)
  between operations  15.2 us (2%)
    all_gather x1, waiting for transfers between devices, local(): lax.all_gather(grad_pad, 'ch', axis=0, tiled=True)  158 us
    all_gather x1, waiting for transfers between devices, local(): lax.all_gather(feat_pad, 'ch', axis=0, tiled=True)  158 us
    all_gather x2, waiting for transfers between devices, face_lines_of(): all_gather(own_rows, axis_name=chip_axis)  86.3 us
    scatter x2, local copies, waits for them, and re-layouts, pad_field(): padded.at[:, :, :, -1]  36.9 us
    select_n x12, local copies, waits for them, and re-layouts, placed(): jnp.where(active, lax.dynamic_update_slice_in_dim(blank, values.astype(jn...  20.3 us
    dot_general x9, matrix products, forward_taps(): jnp.einsum('oc,cfab->ofab', taps[tap_row, tap_col], window, preferred_ele...  18.4 us
    dot_general x9, matrix products, backward_taps(): jnp.einsum('oc,ofab->cfab', taps[tap_row, tap_col], window, preferred_ele...  17.9 us
    ppermute x4, starting transfers between devices, with_halo(): before = lax.ppermute(last, axis, up)  16.4 us
  transfers between devices with their start and end apart: 12, of which 10 were waited for; matrix products, arithmetic and copies ran while one was open for 3% of the time, Pallas kernels for 0%

profile of v1, /device:TPU:8, one launch (start us, length us, event | category | flops | bytes accessed | tf_op | source)
XLA Modules:
  0.0 618.4 jit_solution(6113563107516248471)
XLA Ops:
  7.2 1.4 reshape.684
  9.9 1.4 convert_select_fusion.2
  11.2 3.0 copy.926
  14.2 1.8 copy.927
  16.1 2.7 select_n.206
  18.8 2.7 select_n.210
  25.0 7.1 %collective-permute-start = (bf16[16,12,16,1]{2,0,3,1:T(8,128)(2,1)S(1)}, bf16[16,12,16,1]{2,0,3,1:T(8,128)(2,1)S(1)}, u32[]{:S(2)}, u32[]{:S(2)}) collective-permute-start(bf16[16,12,16,1]{2,0,3,1:T(8,128)(2,1)S(1)} %copy.912), channel_id=1, source_target_pairs={{0,64},{64,128},{128,192},{1,65},{65,129},{129,193},{2,66},{66,130... | collective-permute-start | bytes 18440 | tf_op jit(solution)/shard_map/ppermute | solution.py:17
  37.4 1.6 copy.915
  39.3 1.6 copy.917
  41.6 1.9 collective-permute-start.2
  43.6 3.9 collective-permute-start.3
  49.9 1.6 pad_maximum_fusion
  51.5 44.8 %all-gather.5.cloned.1.call-done = bf16[32,16,12,4,128]{4,1,3,2,0:T(8,128)(2,1)} async-done(((bf16[1,16,12,4,128]{4,1,3,2,0:T(8,128)(2,1)}), bf16[32,16,12,4,128]{4,1,3,2,0:T(8,128)(2,1)}) %all-gather.5.cloned.1.call-update) | async-done | bytes 6291472 | tf_op jit(solution)/shard_map/all_gather | solution.py:77
  96.3 4.3 reduce_sum.24
  108.7 3.8 scatter.30
  116.5 18.3 %scatter.31 = bf16[16,12,18,34]{3,0,2,1:T(8,128)(2,1)S(1)} dynamic-update-slice(bf16[16,12,18,34]{3,0,2,1:T(8,128)(2,1)S(1)} %scatter.30, bf16[16,12,18,1]{3,0,2,1:T(8,128)(2,1)S(1)} %copy.941, s32[]{:T(128)} %constant.293.clone.1, s32[]{:T(128)} %constant.293.clone.1, s32[]{:T(128)} %constant.293.clone.1, s32[]{:T(128)} %constant.308.clone.1) | dynamic-update-slice | bytes 13828 | tf_op jit(solution)/shard_map/scatter | solution.py:101
  136.4 1.3 reshape.699
  137.7 157.8 %all-gather.7.cloned.1.call-done = bf16[128,12,18,34]{3,0,2,1:T(8,128)(2,1)} async-done(((bf16[16,12,18,34]{3,0,2,1:T(8,128)(2,1)}), bf16[128,12,18,34]{3,0,2,1:T(8,128)(2,1)}) %all-gather.7.cloned.1.call-update) | async-done | bytes 1880080 | tf_op jit(solution)/shard_map/all_gather | solution.py:155
  295.5 4.7 fusion.20
  300.4 1.8 fusion.24
  303.1 1.8 fusion.26
  305.8 1.8 fusion.30
  307.6 1.8 fusion.32
  309.5 2.0 fusion.18
  311.4 2.6 fusion.37
  314.0 1.7 convert_select_fusion.1
  316.3 2.3 copy.961
  319.9 1.9 select_n.232
  321.9 1.9 select_n.235
  328.0 5.4 collective-permute-start.4
  337.2 3.4 collective-permute-done.5
  342.0 1.9 collective-permute-start.6
  343.9 3.9 collective-permute-start.7
  348.3 1.5 collective-permute-done.7
  350.5 41.5 %all-gather.9.cloned.1.call-done = bf16[32,16,12,4,128]{4,1,3,2,0:T(8,128)(2,1)} async-done(((bf16[1,16,12,4,128]{4,1,3,2,0:T(8,128)(2,1)}), bf16[32,16,12,4,128]{4,1,3,2,0:T(8,128)(2,1)}) %all-gather.9.cloned.1.call-update) | async-done | bytes 6291472 | tf_op jit(solution)/shard_map/all_gather | solution.py:77
  392.0 4.3 reduce_sum.25
  405.1 3.8 scatter.36
  412.2 18.6 %scatter.39 = bf16[16,12,18,34]{3,0,2,1:T(8,128)(2,1)S(1)} dynamic-update-slice(bf16[16,12,18,34]{3,0,2,1:T(8,128)(2,1)S(1)} %scatter.36, bf16[16,12,18,1]{3,0,2,1:T(8,128)(2,1)S(1)} %copy.975, s32[]{:T(128)} %constant.293.clone.1, s32[]{:T(128)} %constant.293.clone.1, s32[]{:T(128)} %constant.293.clone.1, s32[]{:T(128)} %constant.308.clone.1) | dynamic-update-slice | bytes 13828 | tf_op jit(solution)/shard_map/scatter | solution.py:101
  432.0 1.4 reshape.691
  433.5 158.3 %all-gather.11.cloned.1.call-done = bf16[128,12,18,34]{3,0,2,1:T(8,128)(2,1)} async-done(((bf16[16,12,18,34]{3,0,2,1:T(8,128)(2,1)}), bf16[128,12,18,34]{3,0,2,1:T(8,128)(2,1)}) %all-gather.11.cloned.1.call-update) | async-done | bytes 1880080 | tf_op jit(solution)/shard_map/all_gather | solution.py:162
  591.8 4.8 fusion.2
  597.7 1.9 fusion.10
  600.6 1.9 fusion.14
  602.4 1.9 fusion.4
  604.3 1.9 fusion.8
  606.1 1.3 fusion
  607.5 2.3 add_convert_fusion
  610.0 1.4 reshape.698
  (187 shorter events, 56.7 us)
Async XLA Ops:
  7.2 288.4 %copy-start = (bf16[3,3,128,128]{3,2,1,0:T(8,128)(2,1)S(1)}, bf16[3,3,128,128]{3,2,1,0:T(8,128)(2,1)}, u32[]{:S(2)}) copy-start(bf16[3,3,128,128]{3,2,1,0:T(8,128)(2,1)} %param.27) | copy-start | bytes 884740
  7.2 89.2 %all-gather.5.cloned.1.call-start = ((), (), s32[]{:S(2)}) async-start(), calls=%async_computation | async-start | bytes 6488064 | tf_op jit(solution)/shard_map/all_gather | solution.py:77
  16.0 18.6 %copy-start.15 = (s32[12,4,3]{0,1,2:T(4,128)S(1)}, s32[12,4,3]{0,1,2:T(4,128)}, u32[]{:S(2)}) copy-start(s32[12,4,3]{0,1,2:T(4,128)} %param.28) | copy-start | bytes 1732
  16.0 19.8 %copy-start.24 = (s32[12,4,2]{0,2,1:T(2,128)S(1)}, s32[12,4,2]{0,2,1:T(2,128)}, u32[]{:S(2)}) copy-start(s32[12,4,2]{0,2,1:T(2,128)} %param.29) | copy-start | bytes 1156
  23.8 271.8 %all-gather.7.cloned.1.call-start = ((), (), s32[]{:S(2)}) async-start(), calls=%async_computation.1 | async-start | bytes 7962624 | tf_op jit(solution)/shard_map/all_gather | solution.py:155
  25.0 12.4 %collective-permute-start = (bf16[16,12,16,1]{2,0,3,1:T(8,128)(2,1)S(1)}, bf16[16,12,16,1]{2,0,3,1:T(8,128)(2,1)S(1)}, u32[]{:S(2)}, u32[]{:S(2)}) collective-permute-start(bf16[16,12,16,1]{2,0,3,1:T(8,128)(2,1)S(1)} %copy.912), channel_id=1, source_target_pairs={{0,64},{64,128},{128,192},{1,65},{65,129},{129,193},{2,66},{66,130... | collective-permute-start | bytes 18440 | tf_op jit(solution)/shard_map/ppermute | solution.py:17
  33.3 6.0 collective-permute-start.1
  41.6 6.4 %collective-permute-start.2 = (bf16[16,12,1,34]{3,0,1,2:T(8,128)(2,1)S(1)}, bf16[16,12,1,34]{3,0,1,2:T(8,128)(2,1)S(1)}, u32[]{:S(2)}, u32[]{:S(2)}) collective-permute-start(bf16[16,12,1,34]{3,0,1,2:T(8,128)(2,1)S(1)} %get-tuple-element.146), channel_id=1, source_target_pairs={{0,8},{8,16},{16,24},{24,32},{32,40},{40,48},{48,56},{1,9},{9,17},... | collective-permute-start | bytes 39176 | tf_op jit(solution)/shard_map/ppermute | solution.py:17
  43.6 5.7 collective-permute-start.3
  48.0 1.2 copy-start.8
  49.2 0.6 copy-start.10
  51.5 50.0 %copy-start.13 = (pred[12]{0:T(512)(128)(4,1)S(1)}, pred[12]{0:T(512)(128)(4,1)}, u32[]{:S(2)}) copy-start(pred[12]{0:T(512)(128)(4,1)} %get-tuple-element.172) | copy-start | bytes 40
  51.5 50.9 %copy-start.11 = (pred[12]{0:T(512)(128)(4,1)S(1)}, pred[12]{0:T(512)(128)(4,1)}, u32[]{:S(2)}) copy-start(pred[12]{0:T(512)(128)(4,1)} %get-tuple-element.170) | copy-start | bytes 40
  100.6 4.7 copy-start.18
  100.6 4.8 copy-start.9
  100.7 5.0 copy-start.20
  103.6 3.6 copy-start.22
  112.5 2.5 copy-start.16
  134.9 1.0 copy-start.4
  135.9 256.1 %all-gather.9.cloned.1.call-start = ((), (), s32[]{:S(2)}) async-start(), calls=%async_computation.2 | async-start | bytes 6488064 | tf_op jit(solution)/shard_map/all_gather | solution.py:77
  295.5 4.8 copy-start.2
  326.7 265.1 %all-gather.11.cloned.1.call-start = ((), (), s32[]{:S(2)}) async-start(), calls=%async_computation.3 | async-start | bytes 7962624 | tf_op jit(solution)/shard_map/all_gather | solution.py:162
  328.0 8.0 %collective-permute-start.4 = (bf16[16,12,16,1]{2,0,3,1:T(8,128)(2,1)S(1)}, bf16[16,12,16,1]{2,0,3,1:T(8,128)(2,1)S(1)}, u32[]{:S(2)}, u32[]{:S(2)}) collective-permute-start(bf16[16,12,16,1]{2,0,3,1:T(8,128)(2,1)S(1)} %copy.954), channel_id=1, source_target_pairs={{0,64},{64,128},{128,192},{1,65},{65,129},{129,193},{2,66},{66,130... | collective-permute-start | bytes 18440 | tf_op jit(solution)/shard_map/ppermute | solution.py:17
  334.6 6.0 collective-permute-start.5
  342.0 6.2 %collective-permute-start.6 = (bf16[16,12,1,34]{3,0,2,1:T(8,128)(2,1)S(1)}, bf16[16,12,1,34]{3,0,2,1:T(8,128)(2,1)S(1)}, u32[]{:S(2)}, u32[]{:S(2)}) collective-permute-start(bf16[16,12,1,34]{3,0,2,1:T(8,128)(2,1)S(1)} %get-tuple-element.134), channel_id=1, source_target_pairs={{0,8},{8,16},{16,24},{24,32},{32,40},{40,48},{48,56},{1,9},{9,17},... | collective-permute-start | bytes 39176 | tf_op jit(solution)/shard_map/ppermute | solution.py:17
  343.9 5.8 collective-permute-start.7
  348.3 1.5 copy-start.6
  350.5 48.7 %copy-start.14 = (pred[12]{0:T(512)(128)(4,1)S(1)}, pred[12]{0:T(512)(128)(4,1)}, u32[]{:S(2)}) copy-start(pred[12]{0:T(512)(128)(4,1)} %get-tuple-element.172) | copy-start | bytes 40
  350.5 48.9 %copy-start.23 = (pred[12]{0:T(512)(128)(4,1)S(1)}, pred[12]{0:T(512)(128)(4,1)}, u32[]{:S(2)}) copy-start(pred[12]{0:T(512)(128)(4,1)} %get-tuple-element.168) | copy-start | bytes 40
  350.5 49.0 %copy-start.12 = (pred[12]{0:T(512)(128)(4,1)S(1)}, pred[12]{0:T(512)(128)(4,1)}, u32[]{:S(2)}) copy-start(pred[12]{0:T(512)(128)(4,1)} %get-tuple-element.170) | copy-start | bytes 40
  350.5 49.2 %copy-start.21 = (pred[12]{0:T(512)(128)(4,1)S(1)}, pred[12]{0:T(512)(128)(4,1)}, u32[]{:S(2)}) copy-start(pred[12]{0:T(512)(128)(4,1)} %get-tuple-element.167) | copy-start | bytes 40
  397.0 4.9 copy-start.19
  397.7 4.3 copy-start.7
  408.9 1.8 copy-start.17
  410.9 20.9 %copy-start.5 = (bf16[16,12,16,32]{3,0,2,1:T(8,128)(2,1)S(1)}, bf16[16,12,16,32]{3,0,2,1:T(8,128)(2,1)}, u32[]{:S(2)}) copy-start(bf16[16,12,16,32]{3,0,2,1:T(8,128)(2,1)} %get-tuple-element.137) | copy-start | bytes 589828
  430.8 1.0 copy-start.3
  591.8 4.8 copy-start.1
Sparse Core Ops, SparseCore 0:
  23.9 72.4 all-gather.4
  136.0 159.4 all-gather.6
  326.8 65.1 all-gather.8
  431.9 159.8 all-gather.10
